TPU v7x, 256 devices: a whole 4x4x8 slice. The times are simulated.
256 devices in a mesh: sec: 16 (over z, core), patch: 16 (over x, y).
Axes of the slice: x: 4, y: 4, z: 8, core: 2. Of those that a mesh axis runs over, the one named last changes fastest.
Arguments:
- rhs: bfloat16 [24, 1572864], P(None, ('sec', 'patch')), may hold values from -6 to 6
- curl_blocks: bfloat16 [16384, 4, 9216], P(('sec', 'patch')), may hold values from -0.3125 to 0.3125
- block_cols: int32 [16384, 4], P(('sec', 'patch')), may hold values from 0 to 63
- hole_mask: int32 [16384], P(('sec', 'patch')), may hold values 0 or 1
- edge_flip: int32 [1572864], P(('sec', 'patch')), may hold values from 0 to 1
- send_list: int32 [16, 16, 16, 8], P('sec', 'patch'), may hold values from 0 to 63
- send_count: int32 [16, 16, 16], P('sec', 'patch'), may hold values from 5 to 8
- recv_list: int32 [16, 16, 16, 8], P('sec', 'patch'), may hold values from 0 to 63
- dtn_blocks: bfloat16 [16, 16, 16, 8, 9216], P('sec', 'patch'), may hold values from -0.4375 to 0.4375
Outputs:
- state: float32 [24, 1572864], P(None, ('sec', 'patch'))
Inputs may be any that keep to these rules, and one draw needn't show every extreme that they name: Slots f >= send_count carry no block.
All inputs are finite; a program needn't handle non-finite values. No bound on the sum of `hole_mask` on one device may be relied on, other than what follows from the above.
Results may differ from a plain program's by a relative error of at most 0.029.
Values may be sent and summed in bfloat16 or wider, within the bound.
A program may use at most 64 MiB of HBM per device.

v0:
```python
import jax
import jax.numpy as jnp
from jax import lax
from jax.experimental import pallas as pl
from jax.experimental.pallas import tpu as pltpu
from jax.sharding import PartitionSpec as P

BS = 96
COLS = 24
NB = 64
K = 4
F = 8
NI = 8
ITERS = 8
TICKS = 2
LANES = 128
ROWS = BS * BS // LANES
GROUP = 4
GROUPS = NB // GROUP
PACK = 2 * 3 * COLS
COUPLING = 0.85
CHUNKS = 16
UNROLL = 64

f32 = jnp.float32
bf16 = jnp.bfloat16
NN = (((1,), (0,)), ((), ()))


def lanes_of(shape):
    return lax.broadcasted_iota(jnp.int32, shape, len(shape) - 1)


def split4(a, b, c):
    lane = lanes_of(a.shape)
    return (
        a,
        pltpu.roll(jnp.where(lane >= 96, a, b), 32, 1),
        pltpu.roll(jnp.where(lane >= 64, b, c), 64, 1),
        pltpu.roll(c, 96, 1),
    )


def join4(w, x, y, z):
    lane = lanes_of(w.shape)
    x = pltpu.roll(x, 96, 1)
    y = pltpu.roll(y, 64, 1)
    z = pltpu.roll(z, 32, 1)
    return jnp.where(lane < 96, w, x), jnp.where(lane < 64, x, y), jnp.where(lane < 32, y, z)


def kernel(
    peers, sections,
    rhs, flip, cols, hole, slist, scount, rlist, curl, dtn, out,
    abuf, dbuf, wide, square, mats, dmats, src, frc, img, st0, st1, signed, sign, signrow,
    prod, face, onehot, sendbuf, recvbuf, isend, irecv,
    csem, dsem, ssem, rsem, issem, irsem,
):
    me = lax.axis_index("patch")
    sec = lax.axis_index("sec")

    curl_copies = lambda i: pltpu.make_async_copy(
        curl.at[pl.ds(i * (NB // CHUNKS), NB // CHUNKS)],
        abuf.at[pl.ds(i * (NB // CHUNKS), NB // CHUNKS)],
        csem.at[i],
    )
    dtn_copies = lambda i: pltpu.make_async_copy(dtn.at[i], dbuf.at[i], dsem.at[i])

    irecv[...] = jnp.zeros_like(irecv)
    barrier = pltpu.get_barrier_semaphore()
    for d in range(1, peers):
        pl.semaphore_signal(
            barrier, inc=1, device_id={"patch": lax.rem(me + d, peers)}, device_id_type=pl.DeviceIdType.MESH
        )

    for d in (1, sections - 1):
        pl.semaphore_signal(
            barrier, inc=1, device_id={"sec": lax.rem(sec + d, sections)}, device_id_type=pl.DeviceIdType.MESH
        )

    for i in range(CHUNKS):
        curl_copies(i).start()
    for i in range(peers):
        dtn_copies(i).start()

    signrow[...] = (1 - 2 * flip[...]).astype(f32)
    parts = [signrow[pl.ds(t, GROUPS, stride=3), :] for t in range(3)]
    for r, row in enumerate(split4(*parts)):
        sign[pl.ds(r, GROUPS, stride=4), :] = row

    for i in range(GROUPS):
        parts = [rhs[:, pl.ds(384 * i + LANES * t, LANES)].astype(f32) for t in range(3)]
        for r, row in enumerate(split4(*parts)):
            n = GROUP * i + r
            kept = row * hole[n].astype(f32)
            src[n] = row
            st0[n] = kept.astype(bf16)
            signed[n] = kept * sign[n : n + 1, :]

    pl.semaphore_wait(barrier, peers + 1)

    def face_copy(tick, d):
        return pltpu.make_async_remote_copy(
            src_ref=sendbuf.at[tick, d],
            dst_ref=recvbuf.at[tick, d],
            send_sem=ssem.at[tick, d],
            recv_sem=rsem.at[tick, d],
            device_id={"patch": lax.rem(me + d, peers)},
            device_id_type=pl.DeviceIdType.MESH,
        )

    def packed(q):
        pieces = []
        for half in range(2):
            blocks = []
            for j in range(GROUP):
                f = GROUP * half + j
                used = jnp.where(f < scount[0, q], 1.0, 0.0).astype(f32)
                blocks.append(signed[slist[f, q]] * used)
            pieces.extend(join4(*blocks))
        return jnp.concatenate(pieces, axis=0).astype(bf16)

    def send_faces(tick):
        def one(d, carry):
            sendbuf[tick, d] = packed(lax.rem(me + d, peers))
            face_copy(tick, d).start()
            return carry

        lax.fori_loop(1, peers, one, 0)
        recvbuf[tick, 0] = packed(me)

    def gather(state, n):
        lane = lanes_of((COLS, LANES))
        last = state[cols[3, n]]
        return jnp.concatenate(
            [jnp.where(lane < BS, state[cols[k, n]], pltpu.roll(last, 96 - 32 * k, 1)) for k in range(3)], axis=1
        )

    def image(state, n):
        return lax.dot_general(gather(state, n), mats[n], NN, preferred_element_type=f32)

    def over_blocks(body):
        if UNROLL == NB:
            for store in [body(n) for n in range(NB)]:
                store()
            return

        def batch(i, carry):
            for store in [body(i * UNROLL + u) for u in range(UNROLL)]:
                store()
            return carry

        lax.fori_loop(0, NB // UNROLL, batch, 0)

    def first_image(state):
        def body(n):
            value = image(state, n)

            def store():
                img[n] = value

            return store

        over_blocks(body)

    def sweep(before, after, dtype):
        def body(n):
            value = frc[n] - (COUPLING * hole[n].astype(f32)) * image(before, n)

            def store():
                after[n] = value.astype(dtype)

            return store

        over_blocks(body)

    def relayout_matrices():
        def transposed(base, count, stride, slot):
            parts = [wide[slot, pl.ds(base + stride * t, COLS, stride=3 * stride), :] for t in range(3)]
            for r, row in enumerate(split4(*parts)):
                square[count, pl.ds(r, COLS, stride=4), :] = row
            return lambda: square[count].T[:BS].astype(bf16)

        per = NB // CHUNKS

        def curl_chunk(i, carry):
            curl_copies(i).wait()
            for u in range(per):
                wide[u] = abuf[i * per + u].astype(f32)
            later = [[transposed(k, u * K + k, K, u) for k in range(K)] for u in range(per)]
            for u in range(per):
                n = i * per + u
                for k in range(3):
                    mats[n, LANES * k : LANES * k + BS, :BS] = later[u][k]()
                tail = later[u][3]()
                for k in range(3):
                    mats[n, LANES * k + BS : LANES * (k + 1), :BS] = tail[32 * k : 32 * k + 32]
            return carry

        lax.fori_loop(0, CHUNKS, curl_chunk, 0)

        def dtn_chunk(i, carry):
            for u in range(2):
                dtn_copies(2 * i + u).wait()
            for u in range(2):
                for v in range(2):
                    wide[2 * u + v] = dbuf[2 * i + u, pl.ds(288 * v, 288)].astype(f32)
            later = []
            for u in range(2):
                for f in range(F):
                    parts = []
                    for t in range(3):
                        halves = [
                            wide[2 * u + v, pl.ds(f + F * t, COLS // 2, stride=3 * F), :] for v in range(2)
                        ]
                        parts.append(halves)
                    count = u * F + f
                    for v in range(2):
                        for r, row in enumerate(split4(*[p[v] for p in parts])):
                            square[count, pl.ds(48 * v + r, COLS // 2, stride=4), :] = row
                    later.append(count)
            for u in range(2):
                for f in range(F):
                    dmats[2 * i + u, f, :, :BS] = square[u * F + f].T[:BS].astype(bf16)
            return carry

        lax.fori_loop(0, peers // 2, dtn_chunk, 0)

        lane = lanes_of((1, LANES))
        target = jnp.zeros((1, LANES), jnp.int32)
        for q in range(peers):
            for f in range(F):
                target = jnp.where(lane == q * F + f, rlist[f, q], target)
        rows = lax.broadcasted_iota(jnp.int32, (NB, LANES), 0)
        onehot[...] = jnp.where(rows == target, 1.0, 0.0).astype(bf16)

    def face_products(tick):
        def one(d, carry):
            @pl.when(d > 0)
            def _():
                face_copy(tick, d).wait_recv()

            q = lax.rem(me + peers - d, peers)
            got = recvbuf[tick, d].astype(f32)
            for half in range(2):
                base = 72 * half
                rows = split4(got[base : base + 24], got[base + 24 : base + 48], got[base + 48 : base + 72])
                for j in range(GROUP):
                    f = GROUP * half + j
                    value = lax.dot_general(
                        rows[j].astype(bf16)[:, :BS], dmats[q, f], NN, preferred_element_type=f32
                    )
                    prod[pl.ds(q * F + f, COLS, stride=LANES), :] = value.astype(bf16).astype(f32)
            return carry

        lax.fori_loop(0, peers, one, 0)

        def column(c, carry):
            for u in range(4):
                base = pl.multiple_of((4 * c + u) * LANES, LANES)
                to = pl.multiple_of((4 * c + u) * NB, NB)
                face[pl.ds(to, NB), :] = lax.dot_general(
                    onehot[...], prod[pl.ds(base, LANES), :].astype(bf16), NN, preferred_element_type=f32
                )
            return carry

        lax.fori_loop(0, COLS // 4, column, 0)

    def first_update(tick, after):
        def block(n, extra):
            kept = hole[n].astype(f32)
            forcing = src[n] + face[pl.ds(n, COLS, stride=NB), :]
            if extra is not None:
                forcing = forcing + extra
            forcing = kept * forcing
            frc[n] = forcing
            after[n] = (forcing - (COUPLING * kept) * img[n]).astype(bf16)

        if tick == 0:
            for n in range(NB):
                block(n, None)
        else:
            for side, first in ((0, 0), (1, NB - NI)):
                got = irecv[side].astype(f32)
                for half in range(2):
                    base = 72 * half
                    rows = split4(got[base : base + 24], got[base + 24 : base + 48], got[base + 48 : base + 72])
                    for j in range(GROUP):
                        block(first + GROUP * half + j, rows[j])
            for n in range(NI, NB - NI):
                block(n, None)

    def interface_copy(side):
        return pltpu.make_async_remote_copy(
            src_ref=isend.at[side],
            dst_ref=irecv.at[side],
            send_sem=issem.at[side],
            recv_sem=irsem.at[side],
            device_id={"sec": sec + 1 if side == 0 else sec - 1},
            device_id_type=pl.DeviceIdType.MESH,
        )

    def send_interfaces(state):
        for side, first in ((0, NB - NI), (1, 0)):
            pieces = []
            for half in range(2):
                pieces.extend(join4(*[state[first + GROUP * half + j].astype(f32) for j in range(GROUP)]))
            isend[side] = jnp.concatenate(pieces, axis=0).astype(bf16)

        @pl.when(sec < sections - 1)
        def _():
            interface_copy(0).start()

        @pl.when(sec > 0)
        def _():
            interface_copy(1).start()

    def await_interfaces():
        @pl.when(sec > 0)
        def _():
            interface_copy(0).wait_recv()

        @pl.when(sec < sections - 1)
        def _():
            interface_copy(1).wait_recv()

    def sweeps():
        def pair(i, carry):
            sweep(st1, st0, bf16)
            sweep(st0, st1, bf16)
            return carry

        lax.fori_loop(0, (ITERS - 2) // 2, pair, 0)

    send_faces(0)
    relayout_matrices()
    first_image(st0)
    face_products(0)
    first_update(0, st1)
    sweeps()
    sweep(st1, st0, bf16)

    send_interfaces(st0)
    for n in range(NB):
        signed[n] = st0[n].astype(f32) * sign[n : n + 1, :]
    send_faces(1)
    first_image(st0)
    face_products(1)
    await_interfaces()
    first_update(1, st1)
    sweeps()
    sweep(st1, signed, f32)

    for i in range(GROUPS):
        for t, piece in enumerate(join4(*[signed[GROUP * i + r] for r in range(GROUP)])):
            out[:, pl.ds(384 * i + LANES * t, LANES)] = piece

    for tick in range(TICKS):

        def sent(d, carry):
            face_copy(tick, d).wait_send()
            return carry

        lax.fori_loop(1, peers, sent, 0)

    @pl.when(sec < sections - 1)
    def _():
        interface_copy(0).wait_send()

    @pl.when(sec > 0)
    def _():
        interface_copy(1).wait_send()


def shards(
    rhs, curl_blocks, block_cols, hole_mask, edge_flip, send_list, send_count, recv_list, dtn_blocks
):
    peers = send_list.shape[2]
    sections = lax.axis_size("sec")
    curl = curl_blocks.reshape(NB, K, ROWS, LANES).transpose(0, 2, 1, 3).reshape(NB, K * ROWS, LANES)
    dtn = dtn_blocks[0, 0].reshape(peers, F, ROWS, LANES).transpose(0, 2, 1, 3).reshape(peers, F * ROWS, LANES)
    smem = pl.BlockSpec(memory_space=pltpu.SMEM)
    vmem = pl.BlockSpec(memory_space=pltpu.VMEM)
    hbm = pl.BlockSpec(memory_space=pl.ANY)
    dma = pltpu.SemaphoreType.DMA
    out = pl.pallas_call(
        lambda *refs: kernel(peers, sections, *refs),
        out_shape=jax.ShapeDtypeStruct((COLS, NB * BS), f32),
        in_specs=[vmem, vmem, smem, smem, smem, smem, smem, hbm, hbm],
        out_specs=vmem,
        scratch_shapes=[
            pltpu.VMEM((NB, K * ROWS, LANES), bf16),
            pltpu.VMEM((peers, F * ROWS, LANES), bf16),
            pltpu.VMEM((4, K * ROWS, LANES), f32),
            pltpu.VMEM((16, BS, LANES), f32),
            pltpu.VMEM((NB, 3 * LANES, LANES), bf16),
            pltpu.VMEM((peers, F, BS, LANES), bf16),
            pltpu.VMEM((NB, COLS, LANES), f32),
            pltpu.VMEM((NB, COLS, LANES), f32),
            pltpu.VMEM((NB, COLS, LANES), f32),
            pltpu.VMEM((NB, COLS, LANES), bf16),
            pltpu.VMEM((NB, COLS, LANES), bf16),
            pltpu.VMEM((NB, COLS, LANES), f32),
            pltpu.VMEM((NB, LANES), f32),
            pltpu.VMEM((3 * GROUPS, LANES), f32),
            pltpu.VMEM((COLS * LANES, LANES), f32),
            pltpu.VMEM((COLS * NB, LANES), f32),
            pltpu.VMEM((NB, LANES), bf16),
            pltpu.VMEM((TICKS, peers, PACK, LANES), bf16),
            pltpu.VMEM((TICKS, peers, PACK, LANES), bf16),
            pltpu.VMEM((2, PACK, LANES), bf16),
            pltpu.VMEM((2, PACK, LANES), bf16),
            dma((CHUNKS,)),
            dma((peers,)),
            dma((TICKS, peers)),
            dma((TICKS, peers)),
            dma((2,)),
            dma((2,)),
        ],
        compiler_params=pltpu.CompilerParams(
            collective_id=0, has_side_effects=True, vmem_limit_bytes=56 << 20
        ),
        name="relay",
    )(
        rhs,
        edge_flip.reshape(3 * GROUPS, LANES),
        block_cols.T,
        hole_mask,
        send_list[0, 0].T,
        send_count[0],
        recv_list[0, 0].T,
        curl,
        dtn,
    )
    return out


def solution(mesh):
    in_specs = (
        P(None, ("sec", "patch")),
        P(("sec", "patch"), None, None),
        P(("sec", "patch"), None),
        P(("sec", "patch")),
        P(("sec", "patch")),
        P("sec", "patch", None, None),
        P("sec", "patch", None),
        P("sec", "patch", None, None),
        P("sec", "patch", None, None, None),
    )
    out_specs = P(None, ("sec", "patch"))
    return jax.shard_map(shards, mesh=mesh, in_specs=in_specs, out_specs=out_specs, check_vma=False)
```

profile of v0, /device:TPU:97, one launch (start us, length us, event | category | flops | bytes accessed | tf_op | source)
XLA Modules:
  0.0 61.0 jit_solution(4101487294339367427)
XLA Ops:
  0.0 59.0 %relay.1 = f32[24,6144]{1,0:T(8,128)} custom-call(bf16[24,6144]{1,0:T(8,128)(2,1)} %refs_0_.1, s32[48,128]{1,0:T(8,128)} %bitcast.21, s32[4,64]{1,0:T(4,128)} %bitcast.24, s32[64]{0:T(128)} %refs_3_.1, s32[8,16]{1,0:T(8,128)} %bitcast.22, s32[1,16]{1,0:T(1,128)} %bitcast.25, s32[8,16]{1,0:T(8,128)} %bitcast.23, bf16[64,288,128]{2,1,0:T(8,128)(2,1)} %bitcast.19, ...), custom_call_target="tpu_custom_call" | custom-call | tf_op jit(solution)/shard_map/relay/pallas_call | solution.py:386
  59.0 1.9 %copy.12 = f32[24,6144]{1,0:T(8,128)} copy(f32[24,6144]{1,0:T(8,128)} %relay.1) | data formatting | bytes 1179648
where the time goes:
time: 61.1 us; the launch traced here: 61 us
  Pallas kernels  59 us (97%)
  local copies, waits for them, and re-layouts  1.92 us (3%)
    pallas_call x1, Pallas kernels, shards(): pl.pallas_call(lambda *refs: kernel(peers, sections, *refs), out_shape=ja...  59 us
    unnamed x1, local copies, waits for them, and re-layouts  1.92 us

commit v1 on v0

v1 whole, which is shorter than its diff:
```python
import jax
import jax.numpy as jnp
from jax import lax
from jax.experimental import pallas as pl
from jax.experimental.pallas import tpu as pltpu
from jax.sharding import PartitionSpec as P

BS = 96
COLS = 24
NB = 64
K = 4
F = 8
NI = 8
ITERS = 8
TICKS = 2
LANES = 128
ROWS = BS * BS // LANES
GROUP = 4
GROUPS = NB // GROUP
PACK = 2 * 3 * COLS
COUPLING = 0.85
OCTETS = NB // 8
SIDE = 4
BATCH = 5
ARRIVALS = ((16,), (8, 8))
STEPS = (
    (0, 0), (2, 2), (1, 2), (2, 1), (3, 2), (2, 3), (0, 2), (2, 0),
    (1, 1), (3, 3), (1, 3), (3, 1), (0, 1), (1, 0), (0, 3), (3, 0),
)

f32 = jnp.float32
bf16 = jnp.bfloat16
NN = (((1,), (0,)), ((), ()))


def lanes_of(shape):
    return lax.broadcasted_iota(jnp.int32, shape, len(shape) - 1)


def split4(a, b, c):
    lane = lanes_of(a.shape)
    return (
        a,
        pltpu.roll(jnp.where(lane >= 96, a, b), 32, 1),
        pltpu.roll(jnp.where(lane >= 64, b, c), 64, 1),
        pltpu.roll(c, 96, 1),
    )


def join4(w, x, y, z):
    lane = lanes_of(w.shape)
    x = pltpu.roll(x, 96, 1)
    y = pltpu.roll(y, 64, 1)
    z = pltpu.roll(z, 32, 1)
    return jnp.where(lane < 96, w, x), jnp.where(lane < 64, x, y), jnp.where(lane < 32, y, z)


def kernel(
    peers, sections,
    rhs_in, flip_in, cols, hole, slist, scount, rlist, curl, dtn, out,
    rhs, flip,
    abuf, dbuf, wide, square, dsquare, mats, dmats, src, frc, img, st0, st1, signed, sign, signrow,
    prod, face, onehot, sendbuf, recvbuf, isend, irecv,
    bsem, csem, dsem, ssem, rsem, issem, irsem,
):
    me = lax.axis_index("patch")
    cat = jnp.concatenate
    zeros = jnp.zeros((COLS, LANES), bf16)
    dot = lambda x, y: lax.dot_general(x, y, NN, preferred_element_type=f32)

    def peer(d, sign):
        dx, dy = STEPS[d]
        x = lax.rem(me // SIDE + (dx if sign > 0 else SIDE - dx), SIDE)
        y = lax.rem(lax.rem(me, SIDE) + (dy if sign > 0 else SIDE - dy), SIDE)
        return x * SIDE + y

    sec = lax.axis_index("sec")

    curl_copies = lambda i: pltpu.make_async_copy(
        curl.at[pl.ds(i * 8, 8)],
        abuf.at[pl.ds(i * 8, 8)],
        csem.at[i],
    )
    dtn_copies = lambda i: pltpu.make_async_copy(dtn.at[i], dbuf.at[i], dsem.at[i])

    rhs_copy = pltpu.make_async_copy(rhs_in, rhs, bsem.at[0])
    flip_copy = pltpu.make_async_copy(flip_in, flip, bsem.at[1])
    rhs_copy.start()
    flip_copy.start()
    irecv[...] = jnp.zeros_like(irecv)
    barrier = pltpu.get_barrier_semaphore()
    for d in range(1, peers):
        pl.semaphore_signal(
            barrier, inc=1, device_id={"patch": lax.rem(me + d, peers)}, device_id_type=pl.DeviceIdType.MESH
        )

    for d in (1, sections - 1):
        pl.semaphore_signal(
            barrier, inc=1, device_id={"sec": lax.rem(sec + d, sections)}, device_id_type=pl.DeviceIdType.MESH
        )

    for i in range(OCTETS):
        curl_copies(i).start()
    for i in range(peers):
        dtn_copies(i).start()

    flip_copy.wait()
    signrow[...] = (1 - 2 * flip[...]).astype(f32)
    parts = [signrow[pl.ds(t, GROUPS, stride=3), :] for t in range(3)]
    for r, row in enumerate(split4(*parts)):
        sign[pl.ds(r, GROUPS, stride=4), :] = row

    rhs_copy.wait()
    for i in range(GROUPS):
        parts = [rhs[:, pl.ds(384 * i + LANES * t, LANES)].astype(f32) for t in range(3)]
        for r, row in enumerate(split4(*parts)):
            n = GROUP * i + r
            kept = row * hole[n].astype(f32)
            src[n] = row
            st0[n] = kept.astype(bf16)
            signed[n] = kept * sign[n : n + 1, :]

    pl.semaphore_wait(barrier, peers + 1)

    def face_copy(tick, d):
        return pltpu.make_async_remote_copy(
            src_ref=sendbuf.at[tick, d],
            dst_ref=recvbuf.at[tick, d],
            send_sem=ssem.at[tick, d],
            recv_sem=rsem.at[tick, d],
            device_id={"patch": peer(d, 1)},
            device_id_type=pl.DeviceIdType.MESH,
        )

    def packed(q):
        pieces = []
        for half in range(2):
            blocks = []
            for j in range(GROUP):
                f = GROUP * half + j
                used = jnp.where(f < scount[0, q], 1.0, 0.0).astype(f32)
                blocks.append(signed[slist[f, q]] * used)
            pieces.extend(join4(*blocks))
        return jnp.concatenate(pieces, axis=0).astype(bf16)

    def send_faces(tick):
        for first in range(1, peers, BATCH):
            for d in range(first, first + BATCH):
                sendbuf[tick, d] = packed(peer(d, 1))
            for d in range(first, first + BATCH):
                face_copy(tick, d).start()
        recvbuf[tick, 0] = packed(me)

    def gather(state, n):
        lane = lanes_of((COLS, LANES))
        last = state[cols[3, n]]
        return [jnp.where(lane < BS, state[cols[k, n]], pltpu.roll(last, 96 - 32 * k, 1)) for k in range(3)]

    def images(state, o):
        lane = lanes_of((COLS, LANES))
        xs = [gather(state, 8 * o + i) for i in range(8)]
        front = [cat(x[:2], axis=1) for x in xs]
        low = [cat([x[2], zeros], axis=1) for x in xs[:4]]
        high = [cat([zeros, x[2]], axis=1) for x in xs[4:]]
        first = [
            [dot(cat([front[4 * g + j], front[4 * g + 3]], axis=0), mats[o, 3 * g + j]) for j in range(3)]
            for g in range(2)
        ]
        rest = [dot(cat([low[j], low[3], high[j], high[3]], axis=0), mats[o, 6 + j]) for j in range(3)]
        out = []
        for g in range(2):
            thirds = []
            for j in range(3):
                out.append(first[g][j][:COLS] + rest[j][2 * g * COLS : (2 * g + 1) * COLS])
                third = first[g][j][COLS:] + rest[j][(2 * g + 1) * COLS : (2 * g + 2) * COLS]
                thirds.append(pltpu.roll(third, 32 * j + 32, 1))
            out.append(jnp.where(lane < 32, thirds[0], jnp.where(lane < 64, thirds[1], thirds[2])))
        return out

    def first_image(state):
        values = [images(state, o) for o in range(OCTETS)]
        for o in range(OCTETS):
            for i in range(8):
                img[8 * o + i] = values[o][i]

    def sweep(before, store):
        stores = []
        for o in range(OCTETS):
            for i, value in enumerate(images(before, o)):
                n = 8 * o + i
                stores.append((n, frc[n] - (COUPLING * hole[n].astype(f32)) * value))
        for n, value in stores:
            store(n, value)

    def store_in(ref):
        def store(n, value):
            ref[n] = value.astype(ref.dtype)

        return store

    def store_signed(n, value):
        rounded = value.astype(bf16)
        st0[n] = rounded
        signed[n] = rounded.astype(f32) * sign[n : n + 1, :]

    def relayout_matrices():
        def rows_of(slot, base, stride, count):
            parts = [wide[slot, pl.ds(base + stride * t, count, stride=3 * stride), :] for t in range(3)]
            return split4(*parts)

        def chunk(o, carry):
            lane = lanes_of((COLS // 2, LANES))
            curl_copies(o).wait()
            for u in range(2):
                dtn_copies(2 * o + u).wait()
            for i in range(8):
                wide[i] = abuf[8 * o + i].astype(f32)
            for u in range(2):
                for v in range(2):
                    wide[8 + 2 * u + v] = dbuf[2 * o + u, pl.ds(288 * v, 288)].astype(f32)
            for g in range(2):
                for k in range(K):
                    at = [(g * K + k) * 3 + j for j in range(3)]
                    for j in range(3):
                        for r, row in enumerate(rows_of(4 * g + j, k, K, COLS)):
                            square[at[j], pl.ds(r, COLS, stride=4), :] = row
                    for r, row in enumerate(rows_of(4 * g + 3, k, K, COLS)):
                        for j in range(3):
                            square[at[j], pl.ds(BS + r, 8, stride=4), :] = row[8 * j : 8 * j + 8]
            for u in range(2):
                for f in range(F):
                    for v in range(2):
                        for r, row in enumerate(rows_of(8 + 2 * u + v, f, F, COLS // 2)):
                            row = jnp.where(lane < BS, row, 0.0)
                            dsquare[u * F + f, pl.ds(48 * v + r, COLS // 2, stride=4), :] = row
            for g in range(2):
                for j in range(3):
                    turned = [square[(g * K + k) * 3 + j].T[:BS].astype(bf16) for k in range(K)]
                    mats[o, 3 * g + j] = cat([turned[0], turned[3][:32], turned[1], turned[3][32:64]], axis=0)
                    mats[o, 6 + j, pl.ds(LANES * g, LANES)] = cat([turned[2], turned[3][64:]], axis=0)
            for u in range(2):
                for f in range(F):
                    dmats[2 * o + u, f // 2, pl.ds(LANES * (f % 2), LANES), :BS] = dsquare[u * F + f].T.astype(bf16)
            return carry

        lax.fori_loop(0, OCTETS, chunk, 0)

        lane = lanes_of((1, LANES))
        target = jnp.zeros((1, LANES), jnp.int32)
        for q in range(peers):
            for f in range(F):
                target = jnp.where(lane == q * F + f, rlist[f, q], target)
        rows = lax.broadcasted_iota(jnp.int32, (NB, LANES), 0)
        onehot[...] = jnp.where(rows == target, 1.0, 0.0).astype(bf16)

    def face_product(tick, d):
        q = peer(d, -1)
        got = recvbuf[tick, d].astype(f32)
        for half in range(2):
            base = 72 * half
            rows = split4(got[base : base + 24], got[base + 24 : base + 48], got[base + 48 : base + 72])
            rows = [row.astype(bf16) for row in rows]
            for j in (0, 2):
                f = GROUP * half + j
                both = cat([cat([rows[j], zeros], axis=1), cat([zeros, rows[j + 1]], axis=1)], axis=0)
                value = dot(both, dmats[q, f // 2]).astype(bf16).astype(f32)
                prod[pl.ds(q * F + f, COLS, stride=LANES), :] = value[:COLS]
                prod[pl.ds(q * F + f + 1, COLS, stride=LANES), :] = value[COLS:]

    def face_products(tick):
        begin = 0
        for count in ARRIVALS[tick]:
            for d in range(max(begin, 1), begin + count):
                face_copy(tick, d).wait_recv()
            for d in range(begin, begin + count):
                face_product(tick, d)
            begin += count

        for c in range(COLS):
            face[pl.ds(c * NB, NB), :] = dot(onehot[...], prod[pl.ds(c * LANES, LANES), :].astype(bf16))

    def first_update(tick, after):
        def block(n, extra):
            kept = hole[n].astype(f32)
            forcing = src[n] + face[pl.ds(n, COLS, stride=NB), :]
            if extra is not None:
                forcing = forcing + extra
            forcing = kept * forcing
            frc[n] = forcing
            after[n] = (forcing - (COUPLING * kept) * img[n]).astype(bf16)

        if tick == 0:
            for n in range(NB):
                block(n, None)
        else:
            for side, first in ((0, 0), (1, NB - NI)):
                got = irecv[side].astype(f32)
                for half in range(2):
                    base = 72 * half
                    rows = split4(got[base : base + 24], got[base + 24 : base + 48], got[base + 48 : base + 72])
                    for j in range(GROUP):
                        block(first + GROUP * half + j, rows[j])
            for n in range(NI, NB - NI):
                block(n, None)

    def interface_copy(side):
        return pltpu.make_async_remote_copy(
            src_ref=isend.at[side],
            dst_ref=irecv.at[side],
            send_sem=issem.at[side],
            recv_sem=irsem.at[side],
            device_id={"sec": sec + 1 if side == 0 else sec - 1},
            device_id_type=pl.DeviceIdType.MESH,
        )

    def send_interfaces(state):
        for side, first in ((0, NB - NI), (1, 0)):
            pieces = []
            for half in range(2):
                pieces.extend(join4(*[state[first + GROUP * half + j].astype(f32) for j in range(GROUP)]))
            isend[side] = jnp.concatenate(pieces, axis=0).astype(bf16)

        @pl.when(sec < sections - 1)
        def _():
            interface_copy(0).start()

        @pl.when(sec > 0)
        def _():
            interface_copy(1).start()

    def await_interfaces():
        @pl.when(sec > 0)
        def _():
            interface_copy(0).wait_recv()

        @pl.when(sec < sections - 1)
        def _():
            interface_copy(1).wait_recv()

    def sweeps():
        def pair(i, carry):
            sweep(st1, store_in(st0))
            sweep(st0, store_in(st1))
            return carry

        lax.fori_loop(0, (ITERS - 2) // 2, pair, 0)

    send_faces(0)
    relayout_matrices()
    first_image(st0)
    face_products(0)
    first_update(0, st1)
    sweeps()
    sweep(st1, store_signed)

    send_interfaces(st0)
    send_faces(1)
    first_image(st0)
    face_products(1)
    await_interfaces()
    first_update(1, st1)
    sweeps()
    sweep(st1, store_in(out))

    for tick in range(TICKS):
        for d in range(1, peers):
            face_copy(tick, d).wait_send()

    @pl.when(sec < sections - 1)
    def _():
        interface_copy(0).wait_send()

    @pl.when(sec > 0)
    def _():
        interface_copy(1).wait_send()


def lay_out(state, out):
    for i in range(GROUPS):
        for t, piece in enumerate(join4(*[state[GROUP * i + r] for r in range(GROUP)])):
            out[:, pl.ds(384 * i + LANES * t, LANES)] = piece


def shards(
    rhs, curl_blocks, block_cols, hole_mask, edge_flip, send_list, send_count, recv_list, dtn_blocks
):
    peers = send_list.shape[2]
    sections = lax.axis_size("sec")
    curl = curl_blocks.reshape(NB, K, ROWS, LANES).transpose(0, 2, 1, 3).reshape(NB, K * ROWS, LANES)
    dtn = dtn_blocks[0, 0].reshape(peers, F, ROWS, LANES).transpose(0, 2, 1, 3).reshape(peers, F * ROWS, LANES)
    smem = pl.BlockSpec(memory_space=pltpu.SMEM)
    vmem = pl.BlockSpec(memory_space=pltpu.VMEM)
    hbm = pl.BlockSpec(memory_space=pltpu.HBM)
    dma = pltpu.SemaphoreType.DMA
    state = pl.pallas_call(
        lambda *refs: kernel(peers, sections, *refs),
        out_shape=jax.ShapeDtypeStruct((NB, COLS, LANES), f32),
        in_specs=[hbm, hbm, smem, smem, smem, smem, smem, hbm, hbm],
        out_specs=vmem,
        scratch_shapes=[
            pltpu.VMEM((COLS, NB * BS), bf16),
            pltpu.VMEM((3 * GROUPS, LANES), jnp.int32),
            pltpu.VMEM((NB, K * ROWS, LANES), bf16),
            pltpu.VMEM((peers, F * ROWS, LANES), bf16),
            pltpu.VMEM((12, K * ROWS, LANES), f32),
            pltpu.VMEM((24, LANES, LANES), f32),
            pltpu.VMEM((16, BS, LANES), f32),
            pltpu.VMEM((OCTETS, 9, 2 * LANES, LANES), bf16),
            pltpu.VMEM((peers, F // 2, 2 * LANES, LANES), bf16),
            pltpu.VMEM((NB, COLS, LANES), f32),
            pltpu.VMEM((NB, COLS, LANES), f32),
            pltpu.VMEM((NB, COLS, LANES), f32),
            pltpu.VMEM((NB, COLS, LANES), bf16),
            pltpu.VMEM((NB, COLS, LANES), bf16),
            pltpu.VMEM((NB, COLS, LANES), f32),
            pltpu.VMEM((NB, LANES), f32),
            pltpu.VMEM((3 * GROUPS, LANES), f32),
            pltpu.VMEM((COLS * LANES, LANES), f32),
            pltpu.VMEM((COLS * NB, LANES), f32),
            pltpu.VMEM((NB, LANES), bf16),
            pltpu.VMEM((TICKS, peers, PACK, LANES), bf16),
            pltpu.VMEM((TICKS, peers, PACK, LANES), bf16),
            pltpu.VMEM((2, PACK, LANES), bf16),
            pltpu.VMEM((2, PACK, LANES), bf16),
            dma((2,)),
            dma((OCTETS,)),
            dma((peers,)),
            dma((TICKS, peers)),
            dma((TICKS, peers)),
            dma((2,)),
            dma((2,)),
        ],
        compiler_params=pltpu.CompilerParams(
            collective_id=0, has_side_effects=True, vmem_limit_bytes=52 << 20
        ),
        name="relay",
    )(
        *[
            pltpu.with_memory_space_constraint(x, pltpu.HBM)
            for x in (
                rhs,
                edge_flip.reshape(3 * GROUPS, LANES),
                block_cols.T,
                hole_mask,
                send_list[0, 0].T,
                send_count[0],
                recv_list[0, 0].T,
                curl,
                dtn,
            )
        ]
    )
    return pl.pallas_call(
        lay_out,
        out_shape=jax.ShapeDtypeStruct((COLS, NB * BS), f32),
        in_specs=[vmem],
        out_specs=vmem,
        compiler_params=pltpu.CompilerParams(vmem_limit_bytes=8 << 20),
        name="lay_out",
    )(state)


def solution(mesh):
    in_specs = (
        P(None, ("sec", "patch")),
        P(("sec", "patch"), None, None),
        P(("sec", "patch"), None),
        P(("sec", "patch")),
        P(("sec", "patch")),
        P("sec", "patch", None, None),
        P("sec", "patch", None),
        P("sec", "patch", None, None),
        P("sec", "patch", None, None, None),
    )
    out_specs = P(None, ("sec", "patch"))
    return jax.shard_map(shards, mesh=mesh, in_specs=in_specs, out_specs=out_specs, check_vma=False)
```

time: 61.1 us -> 47.8 us (0.78)
  Pallas kernels: 59 us -> 47.3 us
  local copies, waits for them, and re-layouts: 1.92 us -> 0 us
    pallas_call x1, Pallas kernels: 59 us -> 46.2 us  [shards(): pl.pallas_call(lambda *refs: kernel(peers, sections, *refs), out_shape=ja...]
    unnamed x1 -> x0, local copies, waits for them, and re-layouts: 1.92 us -> none
    pallas_call x0 -> x1, Pallas kernels: none -> 1.03 us  [shards(): pl.pallas_call(lay_out, out_shape=jax.ShapeDtypeStruct((COLS, NB * BS), f...]
where the time goes in v1:
time: 47.8 us; the launch traced here: 47.3 us
  Pallas kernels  47.3 us (99%)
    pallas_call x1, Pallas kernels, shards(): pl.pallas_call(lambda *refs: kernel(peers, sections, *refs), out_shape=ja...  46.2 us
    pallas_call x1, Pallas kernels, shards(): pl.pallas_call(lay_out, out_shape=jax.ShapeDtypeStruct((COLS, NB * BS), f...  1.03 us

profile of v1, /device:TPU:97, one launch (start us, length us, event | category | flops | bytes accessed | tf_op | source)
XLA Modules:
  0.0 47.3 jit_solution(2417323599994706426)
XLA Ops:
  0.0 46.2 %relay.1.state = f32[64,24,128]{2,1,0:T(8,128)S(1)} custom-call(bf16[24,6144]{1,0:T(8,128)(2,1)} %refs_0_.1, s32[48,128]{1,0:T(8,128)} %bitcast.21, s32[4,64]{1,0:T(4,128)} %bitcast.24, s32[64]{0:T(128)} %refs_3_.1, s32[8,16]{1,0:T(8,128)} %bitcast.22, s32[1,16]{1,0:T(1,128)} %bitcast.25, s32[8,16]{1,0:T(8,128)} %bitcast.23, bf16[64,288,128]{2,1,0:T(8,128)(2,1)} %bitcast.19, ...), custom_call_target="tpu_custom_call" | custom-call | tf_op jit(solution)/shard_map/relay/pallas_call | solution.py:395
  46.2 1.0 %lay_out.1 = f32[24,6144]{1,0:T(8,128)} custom-call(f32[64,24,128]{2,1,0:T(8,128)S(1)} %relay.1.state), custom_call_target="tpu_custom_call" | custom-call | tf_op jit(solution)/shard_map/lay_out/pallas_call | solution.py:453

commit v2 on v1

--- a/solution.py
+++ b/solution.py
@@ -21,8 +21,10 @@
 COUPLING = 0.85
 OCTETS = NB // 8
 SIDE = 4
+SLOT_ROWS = 136
+BLOCK_ROWS = 72
 BATCH = 5
-ARRIVALS = ((16,), (8, 8))
+ARRIVALS = ((16,), (8, 5, 3))
 STEPS = (
     (0, 0), (2, 2), (1, 2), (2, 1), (3, 2), (2, 3), (0, 2), (2, 0),
     (1, 1), (3, 3), (1, 3), (3, 1), (0, 1), (1, 0), (0, 3), (3, 0),
@@ -105,7 +107,7 @@
         dtn_copies(i).start()
 
     flip_copy.wait()
-    signrow[...] = (1 - 2 * flip[...]).astype(f32)
+    signrow[: 3 * GROUPS] = (1 - 2 * flip[...]).astype(f32)
     parts = [signrow[pl.ds(t, GROUPS, stride=3), :] for t in range(3)]
     for r, row in enumerate(split4(*parts)):
         sign[pl.ds(r, GROUPS, stride=4), :] = row
@@ -214,10 +216,10 @@
             for u in range(2):
                 dtn_copies(2 * o + u).wait()
             for i in range(8):
-                wide[i] = abuf[8 * o + i].astype(f32)
+                wide[i, : K * ROWS] = abuf[8 * o + i].astype(f32)
             for u in range(2):
                 for v in range(2):
-                    wide[8 + 2 * u + v] = dbuf[2 * o + u, pl.ds(288 * v, 288)].astype(f32)
+                    wide[8 + 2 * u + v, : K * ROWS] = dbuf[2 * o + u, pl.ds(288 * v, 288)].astype(f32)
             for g in range(2):
                 for k in range(K):
                     at = [(g * K + k) * 3 + j for j in range(3)]
@@ -235,12 +237,12 @@
                             dsquare[u * F + f, pl.ds(48 * v + r, COLS // 2, stride=4), :] = row
             for g in range(2):
                 for j in range(3):
-                    turned = [square[(g * K + k) * 3 + j].T[:BS].astype(bf16) for k in range(K)]
+                    turned = [square[(g * K + k) * 3 + j, :LANES].T[:BS].astype(bf16) for k in range(K)]
                     mats[o, 3 * g + j] = cat([turned[0], turned[3][:32], turned[1], turned[3][32:64]], axis=0)
                     mats[o, 6 + j, pl.ds(LANES * g, LANES)] = cat([turned[2], turned[3][64:]], axis=0)
             for u in range(2):
                 for f in range(F):
-                    dmats[2 * o + u, f // 2, pl.ds(LANES * (f % 2), LANES), :BS] = dsquare[u * F + f].T.astype(bf16)
+                    dmats[2 * o + u, f // 2, pl.ds(LANES * (f % 2), LANES), :BS] = dsquare[u * F + f, :BS].T.astype(bf16)
             return carry
 
         lax.fori_loop(0, OCTETS, chunk, 0)
@@ -264,8 +266,8 @@
                 f = GROUP * half + j
                 both = cat([cat([rows[j], zeros], axis=1), cat([zeros, rows[j + 1]], axis=1)], axis=0)
                 value = dot(both, dmats[q, f // 2]).astype(bf16).astype(f32)
-                prod[pl.ds(q * F + f, COLS, stride=LANES), :] = value[:COLS]
-                prod[pl.ds(q * F + f + 1, COLS, stride=LANES), :] = value[COLS:]
+                prod[pl.ds(q * F + f, COLS, stride=SLOT_ROWS), :] = value[:COLS]
+                prod[pl.ds(q * F + f + 1, COLS, stride=SLOT_ROWS), :] = value[COLS:]
 
     def face_products(tick):
         begin = 0
@@ -277,12 +279,14 @@
             begin += count
 
         for c in range(COLS):
-            face[pl.ds(c * NB, NB), :] = dot(onehot[...], prod[pl.ds(c * LANES, LANES), :].astype(bf16))
+            face[pl.ds(c * BLOCK_ROWS, NB), :] = dot(
+                onehot[...], prod[pl.ds(c * SLOT_ROWS, LANES), :].astype(bf16)
+            )
 
     def first_update(tick, after):
         def block(n, extra):
             kept = hole[n].astype(f32)
-            forcing = src[n] + face[pl.ds(n, COLS, stride=NB), :]
+            forcing = src[n] + face[pl.ds(n, COLS, stride=BLOCK_ROWS), :]
             if extra is not None:
                 forcing = forcing + extra
             forcing = kept * forcing
@@ -402,9 +406,9 @@
             pltpu.VMEM((3 * GROUPS, LANES), jnp.int32),
             pltpu.VMEM((NB, K * ROWS, LANES), bf16),
             pltpu.VMEM((peers, F * ROWS, LANES), bf16),
-            pltpu.VMEM((12, K * ROWS, LANES), f32),
-            pltpu.VMEM((24, LANES, LANES), f32),
-            pltpu.VMEM((16, BS, LANES), f32),
+            pltpu.VMEM((12, 408, LANES), f32),
+            pltpu.VMEM((24, LANES + 8, LANES), f32),
+            pltpu.VMEM((16, 120, LANES), f32),
             pltpu.VMEM((OCTETS, 9, 2 * LANES, LANES), bf16),
             pltpu.VMEM((peers, F // 2, 2 * LANES, LANES), bf16),
             pltpu.VMEM((NB, COLS, LANES), f32),
@@ -413,10 +417,10 @@
             pltpu.VMEM((NB, COLS, LANES), bf16),
             pltpu.VMEM((NB, COLS, LANES), bf16),
             pltpu.VMEM((NB, COLS, LANES), f32),
-            pltpu.VMEM((NB, LANES), f32),
-            pltpu.VMEM((3 * GROUPS, LANES), f32),
-            pltpu.VMEM((COLS * LANES, LANES), f32),
-            pltpu.VMEM((COLS * NB, LANES), f32),
+            pltpu.VMEM((NB + 8, LANES), f32),
+            pltpu.VMEM((3 * GROUPS + 8, LANES), f32),
+            pltpu.VMEM(((COLS + 1) * SLOT_ROWS, LANES), f32),
+            pltpu.VMEM(((COLS + 1) * BLOCK_ROWS, LANES), f32),
             pltpu.VMEM((NB, LANES), bf16),
             pltpu.VMEM((TICKS, peers, PACK, LANES), bf16),
             pltpu.VMEM((TICKS, peers, PACK, LANES), bf16),

time: 47.8 us -> 45.6 us (0.954)
  Pallas kernels: 47.3 us -> 45.3 us
    pallas_call x1, Pallas kernels: 46.2 us -> 44.2 us  [shards(): pl.pallas_call(lambda *refs: kernel(peers, sections, *refs), out_shape=ja...]
where the time goes in v2:
time: 45.6 us; the launch traced here: 45.3 us
  Pallas kernels  45.3 us (99%)
    pallas_call x1, Pallas kernels, shards(): pl.pallas_call(lambda *refs: kernel(peers, sections, *refs), out_shape=ja...  44.2 us
    pallas_call x1, Pallas kernels, shards(): pl.pallas_call(lay_out, out_shape=jax.ShapeDtypeStruct((COLS, NB * BS), f...  1.03 us

profile of v2, /device:TPU:97, one launch (start us, length us, event | category | flops | bytes accessed | tf_op | source)
XLA Modules:
  0.0 45.3 jit_solution(12742723400737872253)
XLA Ops:
  0.0 44.2 %relay.1.state = f32[64,24,128]{2,1,0:T(8,128)S(1)} custom-call(bf16[24,6144]{1,0:T(8,128)(2,1)} %refs_0_.1, s32[48,128]{1,0:T(8,128)} %bitcast.21, s32[4,64]{1,0:T(4,128)} %bitcast.24, s32[64]{0:T(128)} %refs_3_.1, s32[8,16]{1,0:T(8,128)} %bitcast.22, s32[1,16]{1,0:T(1,128)} %bitcast.25, s32[8,16]{1,0:T(8,128)} %bitcast.23, bf16[64,288,128]{2,1,0:T(8,128)(2,1)} %bitcast.19, ...), custom_call_target="tpu_custom_call" | custom-call | tf_op jit(solution)/shard_map/relay/pallas_call | solution.py:399
  44.2 1.0 %lay_out.1 = f32[24,6144]{1,0:T(8,128)} custom-call(f32[64,24,128]{2,1,0:T(8,128)S(1)} %relay.1.state), custom_call_target="tpu_custom_call" | custom-call | tf_op jit(solution)/shard_map/lay_out/pallas_call | solution.py:457
